TPU v7x, 32 devices: a whole 2x2x4 slice. The times are simulated.
32 devices in a mesh: region: 2 (over x), rows: 8 (over z, y), section: 2 (over core).
Axes of the slice: x: 2, y: 2, z: 4, core: 2. Of those that a mesh axis runs over, the one named last changes fastest.
Arguments:
- transitions: float32 [4, 4, 4096, 4096], P(('region', 'section'), None, 'rows'), parts along dimension 0, may hold values from 0 to 1, as said below
- gain: float32 [4, 4, 4096], P(('region', 'section'), None, 'rows'), parts along dimension 0, may hold values from 0 to 1
- cost: float32 [4, 4, 8], P(('region', 'section')), parts along dimension 0, may hold values from 0 to 1
- price_class: int32 [2048], P('region'), parts along dimension 0, may hold values from 0 to 7
- terminal: float32 [8192, 1024], P(('region', 'rows')), parts along dimension 0, may hold values from 0.5 to 3.5
Outputs:
- values: float32 [4, 4096, 1024], P(('region', 'section'), 'rows'), parts along dimension 0
There are 2 independent parts, one for each index of `region`. A program takes and returns all parts, laid end to end along the dimension named above; each array names one. Nothing has to cross between parts.
Inputs may be any that keep to these rules, and one draw needn't show every extreme that they name: `transitions`: entries are nonnegative.
All inputs are finite; a program needn't handle non-finite values.
Results may differ from a plain program's by a relative error of at most 0.0001.
Values sent between devices are 32-bit elements; how exact they have to be, the bound alone decides.
No kernel may reach another device: no remote copies, remote signals or barrier semaphores. Data moves between devices by JAX's collectives and lax.ppermute only.
A program may use at most 128 MiB of HBM per device.

v0:
```python
import jax
import jax.numpy as jnp
from jax import lax
from jax.sharding import PartitionSpec as P


def from_behind(value, axis, by):
    size = lax.axis_size(axis)
    pairs = [(i, i + by) for i in range(size) if 0 <= i + by < size]
    return lax.ppermute(value, axis, pairs)


def shards(transitions, gain, cost, price_class, terminal):
    num_groups = lax.axis_size("section")
    my_group = lax.axis_index("section")
    kernel = transitions[0]
    action_count, rows_here, state_count = kernel.shape
    scenarios = terminal.shape[1]
    price_levels = cost.shape[2]
    batch_count = 4
    batch_width = scenarios // batch_count
    levels = jnp.arange(price_levels, dtype=jnp.int32)
    onehot = (price_class[None, :] == levels[:, None]).astype(jnp.float32)
    charge = jnp.dot(cost[0], onehot, precision=lax.Precision.HIGHEST)
    gains = gain[0]
    is_last = my_group == num_groups - 1

    def accumulate(panel):
        return jnp.einsum(
            "arn,nc->arc",
            kernel,
            panel,
            precision=lax.Precision.HIGHEST,
            preferred_element_type=jnp.float32,
        )

    def advance(step_index, carry):
        incoming, results = carry
        batch_index = step_index - (num_groups - 1 - my_group)
        is_live = (batch_index >= 0) & (batch_index < batch_count)
        clamped = jnp.clip(batch_index, 0, batch_count - 1)
        first_col = clamped * batch_width
        from_end = lax.dynamic_slice_in_dim(terminal, first_col, batch_width, 1)
        current = jnp.where(is_last, from_end, incoming)
        summed = accumulate(lax.all_gather(current, "rows", axis=0, tiled=True))
        batch_charge = lax.dynamic_slice_in_dim(charge, first_col, batch_width, 1)
        action_value = summed + gains[:, :, None] - batch_charge[:, None, :]
        values_now = jnp.max(action_value, axis=0)
        previous = lax.dynamic_slice_in_dim(results, first_col, batch_width, 1)
        results = lax.dynamic_update_slice_in_dim(
            results, jnp.where(is_live, values_now, previous), first_col, 1
        )
        handed = from_behind(values_now, "section", -1)
        return (handed, results)

    step_total = batch_count + num_groups - 1
    start_carry = (
        jnp.zeros((rows_here, batch_width), jnp.float32),
        jnp.zeros((rows_here, scenarios), jnp.float32),
    )
    final_carry = lax.fori_loop(0, step_total, advance, start_carry)
    return final_carry[1][None]


def solution(mesh):
    return jax.shard_map(
        shards,
        mesh=mesh,
        in_specs=(
            P(("region", "section"), None, "rows", None),
            P(("region", "section"), None, "rows"),
            P(("region", "section"), None, None),
            P("region"),
            P(("region", "rows"), None),
        ),
        out_specs=P(("region", "section"), "rows", None),
        check_vma=False,
    )
```

profile of v0, /device:TPU:1, one launch (start us, length us, event | category | flops | bytes accessed | tf_op | source)
XLA Modules:
  0.0 578.3 jit_solution(10681932668837966376)
XLA Ops:
  6.5 0.7 copy-done
  7.2 0.8 convolution_bitcast_fusion
  8.0 0.1 broadcast_in_dim.14
  8.1 1.6 broadcast_in_dim.15.clone
  9.7 562.0 %while.17 = (s32[]{:T(128)}, f32[512,256]{0,1:T(8,128)S(1)}, f32[512,1024]{1,0:T(8,128)}, pred[]{:T(512)}, s32[]{:T(128)}, /*index=5*/f32[512,1024]{1,0:T(8,128)...) while((s32[]{:T(128)}, f32[512,256]{0,1:T(8,128)S(1)}, ...), condition=%wide.region_2.3_spmd, body=%wide.region_0.2_spmd.sunk | while | flops 25771507712 | bytes 63983956 | solution.py:61
  9.7 1.1 constant_dynamic-slice_fusion.6
  10.8 0.2 copy.17
  11.0 0.9 broadcast_select_fusion.4
  11.9 0.0 all-gather.2.cloned.1.call-update
  11.9 75.1 %all-gather.2.cloned.1.call-done = f32[4096,256]{0,1:T(8,128)} async-done(((f32[512,256]{0,1:T(8,128)}), f32[4096,256]{0,1:T(8,128)}) %all-gather.2.cloned.1.call-update) | async-done | bytes 4194320 | tf_op jit(solution)/shard_map/while/body/eval_jaxpr/all_gather | solution.py:45
  87.0 32.4 %fusion.13 = f32[512,256]{0,1:T(8,128)S(1)} fusion(f32[4,512,4096]{2,1,0:T(8,128)} %get-tuple-element.345, f32[4096,256]{0,1:T(8,128)} %all-gather.2.cloned.1.call-done, f32[4,256]{1,0:T(4,128)S(1)} %constant_dynamic-slice_fusion.7, f32[4,512]{1,0:T(4,128)S(1)} %bitcast.27), kind=kOutput, calls=%fused_computation.3.clone.1 | convolution fusion | flops 25771245568 | bytes 38285312 | tf_op jit(solution)/shard_map/while/body/eval_jaxpr/arn,nc->arc/dot_general | solution.py:29
  119.4 3.8 collective-permute-start
  123.3 1.1 constant_dynamic-slice_fusion.8
  124.3 0.2 copy.18
  124.5 0.1 broadcast_select_fusion.5
  124.6 0.2 copy.19
  124.8 0.8 constant_dynamic-update-slice_fusion.2
  125.7 1.1 constant_dynamic-slice_fusion.6
  126.8 0.2 copy.17
  127.0 0.9 broadcast_select_fusion.4
  127.9 0.0 all-gather.2.cloned.1.call-update
  127.9 70.8 %all-gather.2.cloned.1.call-done = f32[4096,256]{0,1:T(8,128)} async-done(((f32[512,256]{0,1:T(8,128)}), f32[4096,256]{0,1:T(8,128)}) %all-gather.2.cloned.1.call-update) | async-done | bytes 4194320 | tf_op jit(solution)/shard_map/while/body/eval_jaxpr/all_gather | solution.py:45
  198.7 32.4 %fusion.13 = f32[512,256]{0,1:T(8,128)S(1)} fusion(f32[4,512,4096]{2,1,0:T(8,128)} %get-tuple-element.345, f32[4096,256]{0,1:T(8,128)} %all-gather.2.cloned.1.call-done, f32[4,256]{1,0:T(4,128)S(1)} %constant_dynamic-slice_fusion.7, f32[4,512]{1,0:T(4,128)S(1)} %bitcast.27), kind=kOutput, calls=%fused_computation.3.clone.1 | convolution fusion | flops 25771245568 | bytes 38285312 | tf_op jit(solution)/shard_map/while/body/eval_jaxpr/arn,nc->arc/dot_general | solution.py:29
  231.1 3.8 collective-permute-start
  234.9 1.1 constant_dynamic-slice_fusion.8
  236.0 0.2 copy.18
  236.2 0.1 broadcast_select_fusion.5
  236.3 0.2 copy.19
  236.5 0.8 constant_dynamic-update-slice_fusion.2
  237.4 1.1 constant_dynamic-slice_fusion.6
  238.4 0.2 copy.17
  238.6 0.9 broadcast_select_fusion.4
  239.5 0.0 all-gather.2.cloned.1.call-update
  239.6 70.8 %all-gather.2.cloned.1.call-done = f32[4096,256]{0,1:T(8,128)} async-done(((f32[512,256]{0,1:T(8,128)}), f32[4096,256]{0,1:T(8,128)}) %all-gather.2.cloned.1.call-update) | async-done | bytes 4194320 | tf_op jit(solution)/shard_map/while/body/eval_jaxpr/all_gather | solution.py:45
  310.3 32.4 %fusion.13 = f32[512,256]{0,1:T(8,128)S(1)} fusion(f32[4,512,4096]{2,1,0:T(8,128)} %get-tuple-element.345, f32[4096,256]{0,1:T(8,128)} %all-gather.2.cloned.1.call-done, f32[4,256]{1,0:T(4,128)S(1)} %constant_dynamic-slice_fusion.7, f32[4,512]{1,0:T(4,128)S(1)} %bitcast.27), kind=kOutput, calls=%fused_computation.3.clone.1 | convolution fusion | flops 25771245568 | bytes 38285312 | tf_op jit(solution)/shard_map/while/body/eval_jaxpr/arn,nc->arc/dot_general | solution.py:29
  342.8 3.8 collective-permute-start
  346.6 1.1 constant_dynamic-slice_fusion.8
  347.7 0.2 copy.18
  347.9 0.1 broadcast_select_fusion.5
  348.0 0.2 copy.19
  348.2 0.8 constant_dynamic-update-slice_fusion.2
  349.0 1.1 constant_dynamic-slice_fusion.6
  350.1 0.2 copy.17
  350.3 0.9 broadcast_select_fusion.4
  351.2 0.0 all-gather.2.cloned.1.call-update
  351.2 70.4 %all-gather.2.cloned.1.call-done = f32[4096,256]{0,1:T(8,128)} async-done(((f32[512,256]{0,1:T(8,128)}), f32[4096,256]{0,1:T(8,128)}) %all-gather.2.cloned.1.call-update) | async-done | bytes 4194320 | tf_op jit(solution)/shard_map/while/body/eval_jaxpr/all_gather | solution.py:45
  421.7 32.4 %fusion.13 = f32[512,256]{0,1:T(8,128)S(1)} fusion(f32[4,512,4096]{2,1,0:T(8,128)} %get-tuple-element.345, f32[4096,256]{0,1:T(8,128)} %all-gather.2.cloned.1.call-done, f32[4,256]{1,0:T(4,128)S(1)} %constant_dynamic-slice_fusion.7, f32[4,512]{1,0:T(4,128)S(1)} %bitcast.27), kind=kOutput, calls=%fused_computation.3.clone.1 | convolution fusion | flops 25771245568 | bytes 38285312 | tf_op jit(solution)/shard_map/while/body/eval_jaxpr/arn,nc->arc/dot_general | solution.py:29
  454.1 3.8 collective-permute-start
  457.9 1.1 constant_dynamic-slice_fusion.8
  459.0 0.2 copy.18
  459.2 0.1 broadcast_select_fusion.5
  459.3 0.2 copy.19
  459.5 0.8 constant_dynamic-update-slice_fusion.2
  460.4 1.1 constant_dynamic-slice_fusion.6
  461.5 0.2 copy.17
  461.7 0.9 broadcast_select_fusion.4
  462.6 70.4 %all-gather.2.cloned.1.call-done = f32[4096,256]{0,1:T(8,128)} async-done(((f32[512,256]{0,1:T(8,128)}), f32[4096,256]{0,1:T(8,128)}) %all-gather.2.cloned.1.call-update) | async-done | bytes 4194320 | tf_op jit(solution)/shard_map/while/body/eval_jaxpr/all_gather | solution.py:45
  533.0 32.4 %fusion.13 = f32[512,256]{0,1:T(8,128)S(1)} fusion(f32[4,512,4096]{2,1,0:T(8,128)} %get-tuple-element.345, f32[4096,256]{0,1:T(8,128)} %all-gather.2.cloned.1.call-done, f32[4,256]{1,0:T(4,128)S(1)} %constant_dynamic-slice_fusion.7, f32[4,512]{1,0:T(4,128)S(1)} %bitcast.27), kind=kOutput, calls=%fused_computation.3.clone.1 | convolution fusion | flops 25771245568 | bytes 38285312 | tf_op jit(solution)/shard_map/while/body/eval_jaxpr/arn,nc->arc/dot_general | solution.py:29
  565.5 3.8 collective-permute-start
  569.3 1.1 constant_dynamic-slice_fusion.8
  570.4 0.2 copy.18
  570.6 0.1 broadcast_select_fusion.5
  570.7 0.2 copy.19
  570.9 0.8 constant_dynamic-update-slice_fusion.2
  (19 shorter events, 0.1 us)
Async XLA Ops:
  6.5 0.7 copy-start
  6.5 3.1 copy-start.1
  9.7 77.3 %all-gather.2.cloned.1.call-start = ((), (), s32[]{:S(2)}) async-start(), calls=%async_computation | async-start | bytes 4718592 | tf_op jit(solution)/shard_map/while/body/eval_jaxpr/all_gather | solution.py:45
  119.4 6.2 %collective-permute-start = (f32[512,256]{0,1:T(8,128)S(1)}, f32[512,256]{0,1:T(8,128)S(1)}, u32[]{:S(2)}, u32[]{:S(2)}) collective-permute-start(f32[512,256]{0,1:T(8,128)S(1)} %fusion.13), channel_id=1, source_target_pairs={{1,0},{3,2},{5,4},{7,6},{9,8},{11,10},{13,12},{15,14},{17,16},{19,... | collective-permute-start | bytes 1572872 | tf_op jit(solution)/shard_map/while/body/eval_jaxpr/ppermute | solution.py:10
  125.7 73.0 %all-gather.2.cloned.1.call-start = ((), (), s32[]{:S(2)}) async-start(), calls=%async_computation | async-start | bytes 4718592 | tf_op jit(solution)/shard_map/while/body/eval_jaxpr/all_gather | solution.py:45
  231.1 6.2 %collective-permute-start = (f32[512,256]{0,1:T(8,128)S(1)}, f32[512,256]{0,1:T(8,128)S(1)}, u32[]{:S(2)}, u32[]{:S(2)}) collective-permute-start(f32[512,256]{0,1:T(8,128)S(1)} %fusion.13), channel_id=1, source_target_pairs={{1,0},{3,2},{5,4},{7,6},{9,8},{11,10},{13,12},{15,14},{17,16},{19,... | collective-permute-start | bytes 1572872 | tf_op jit(solution)/shard_map/while/body/eval_jaxpr/ppermute | solution.py:10
  237.4 73.0 %all-gather.2.cloned.1.call-start = ((), (), s32[]{:S(2)}) async-start(), calls=%async_computation | async-start | bytes 4718592 | tf_op jit(solution)/shard_map/while/body/eval_jaxpr/all_gather | solution.py:45
  342.8 6.2 %collective-permute-start = (f32[512,256]{0,1:T(8,128)S(1)}, f32[512,256]{0,1:T(8,128)S(1)}, u32[]{:S(2)}, u32[]{:S(2)}) collective-permute-start(f32[512,256]{0,1:T(8,128)S(1)} %fusion.13), channel_id=1, source_target_pairs={{1,0},{3,2},{5,4},{7,6},{9,8},{11,10},{13,12},{15,14},{17,16},{19,... | collective-permute-start | bytes 1572872 | tf_op jit(solution)/shard_map/while/body/eval_jaxpr/ppermute | solution.py:10
  349.0 72.7 %all-gather.2.cloned.1.call-start = ((), (), s32[]{:S(2)}) async-start(), calls=%async_computation | async-start | bytes 4718592 | tf_op jit(solution)/shard_map/while/body/eval_jaxpr/all_gather | solution.py:45
  454.1 6.2 %collective-permute-start = (f32[512,256]{0,1:T(8,128)S(1)}, f32[512,256]{0,1:T(8,128)S(1)}, u32[]{:S(2)}, u32[]{:S(2)}) collective-permute-start(f32[512,256]{0,1:T(8,128)S(1)} %fusion.13), channel_id=1, source_target_pairs={{1,0},{3,2},{5,4},{7,6},{9,8},{11,10},{13,12},{15,14},{17,16},{19,... | collective-permute-start | bytes 1572872 | tf_op jit(solution)/shard_map/while/body/eval_jaxpr/ppermute | solution.py:10
  460.4 72.7 %all-gather.2.cloned.1.call-start = ((), (), s32[]{:S(2)}) async-start(), calls=%async_computation | async-start | bytes 4718592 | tf_op jit(solution)/shard_map/while/body/eval_jaxpr/all_gather | solution.py:45
  565.5 6.2 %collective-permute-start = (f32[512,256]{0,1:T(8,128)S(1)}, f32[512,256]{0,1:T(8,128)S(1)}, u32[]{:S(2)}, u32[]{:S(2)}) collective-permute-start(f32[512,256]{0,1:T(8,128)S(1)} %fusion.13), channel_id=1, source_target_pairs={{1,0},{3,2},{5,4},{7,6},{9,8},{11,10},{13,12},{15,14},{17,16},{19,... | collective-permute-start | bytes 1572872 | tf_op jit(solution)/shard_map/while/body/eval_jaxpr/ppermute | solution.py:10
Sparse Core Ops, SparseCore 0:
  12.7 74.2 all-gather.1
  128.7 69.9 all-gather.1
  240.4 69.9 all-gather.1
  351.7 69.9 all-gather.1
  463.1 69.9 all-gather.1
where the time goes:
time: 579 us; the launch traced here: 578 us
  waiting for transfers between devices  358 us (62%)
  matrix products  163 us (28%)
  local copies, waits for them, and re-layouts  20.3 us (4%)
  starting transfers between devices  19 us (3%)
  between operations  13.1 us (2%)
    all_gather x5, waiting for transfers between devices, advance(): summed = accumulate(lax.all_gather(current, 'rows', axis=0, tiled=True))  357 us
    dot_general x5, matrix products, accumulate(): jnp.einsum('arn,nc->arc', kernel, panel, precision=lax.Precision.HIGHEST,...  162 us
    ppermute x5, starting transfers between devices, from_behind(): return lax.ppermute(value, axis, pairs)  19 us
  transfers between devices with their start and end apart: 10, of which 5 were waited for; matrix products, arithmetic and copies ran while one was open for 2% of the time, Pallas kernels for 0%

commit v1 on v0

--- a/solution.py
+++ b/solution.py
@@ -42,7 +42,28 @@
         first_col = clamped * batch_width
         from_end = lax.dynamic_slice_in_dim(terminal, first_col, batch_width, 1)
         current = jnp.where(is_last, from_end, incoming)
-        summed = accumulate(lax.all_gather(current, "rows", axis=0, tiled=True))
+
+        def treat_surface(u, dimension_no):
+            axis_key = "rows"
+            n = lax.psum(1, axis_name=axis_key)
+            grid = tuple(((c, (c + 1) % n) for c in range(n)))
+            reached, now = ([u], [u])
+            bank = tuple(((c, (c - 1) % n) for c in range(n)))
+            for _ in range(n // 2):
+                reached.append(lax.ppermute(reached[-1], axis_name=axis_key, perm=grid))
+            dd = 0
+            while dd < (n - 1) // 2:
+                now.append(lax.ppermute(now[-1], axis_name=axis_key, perm=bank))
+                dd += 1
+            s_next = jnp.concatenate([*reached[::-1], *now[1:]], axis=dimension_no)
+            passed = jnp.roll(
+                s_next,
+                (lax.axis_index(axis_key) - n // 2) * u.shape[dimension_no],
+                axis=dimension_no,
+            )
+            return passed
+
+        summed = accumulate(treat_surface(current, 0))
         batch_charge = lax.dynamic_slice_in_dim(charge, first_col, batch_width, 1)
         action_value = summed + gains[:, :, None] - batch_charge[:, None, :]
         values_now = jnp.max(action_value, axis=0)

time: 579 us -> 664 us (1.15)
  starting transfers between devices: 19 us -> 107 us
  local copies, waits for them, and re-layouts: 20.3 us -> 34.4 us
  between operations: 13.1 us -> 0.01 us
    all_gather x5 -> x0, waiting for transfers between devices: 357 us -> none  [advance(): summed = accumulate(lax.all_gather(current, 'rows', axis=0, tiled=True))]
    ppermute x0 -> x35, waiting for transfers between devices: none -> 355 us  [the longest x20 342 us: treat_surface(): reached.append(lax.ppermute(reached[-1], axis_name=axis_key, perm=grid))]
    ppermute x0 -> x35, starting transfers between devices: none -> 90.4 us  [the longest x15 61.7 us: treat_surface(): now.append(lax.ppermute(now[-1], axis_name=axis_key, perm=bank))]
    while x0 -> x85, local copies, waits for them, and re-layouts: none -> 13.2 us
  transfers between devices with their start and end apart: 10 -> 40, of which waited for: 5 -> 30; matrix products, arithmetic and copies ran while one was open for 2% -> 3% of each run, Pallas kernels for 0% -> 0%
where the time goes in v1:
time: 664 us; the launch traced here: 663 us
  waiting for transfers between devices  355 us (53%)
  matrix products  165 us (25%)
  starting transfers between devices  107 us (16%)
  local copies, waits for them, and re-layouts  34.4 us (5%)
    ppermute x20, waiting for transfers between devices, treat_surface(): reached.append(lax.ppermute(reached[-1], axis_name=axis_key, perm=grid))  342 us
    dot_general x5, matrix products, accumulate(): jnp.einsum('arn,nc->arc', kernel, panel, precision=lax.Precision.HIGHEST,...  164 us
    ppermute x15, starting transfers between devices, treat_surface(): now.append(lax.ppermute(now[-1], axis_name=axis_key, perm=bank))  61.7 us
    ppermute x20, starting transfers between devices, treat_surface(): reached.append(lax.ppermute(reached[-1], axis_name=axis_key, perm=grid))  28.6 us
    ppermute x5, starting transfers between devices, from_behind(): return lax.ppermute(value, axis, pairs)  16.6 us
  transfers between devices with their start and end apart: 40, of which 30 were waited for; matrix products, arithmetic and copies ran while one was open for 3% of the time, Pallas kernels for 0%

profile of v1, /device:TPU:1, one launch (start us, length us, event | category | flops | bytes accessed | tf_op | source)
XLA Modules:
  0.0 663.0 jit_solution(5300821813988938035)
XLA Ops:
  1.5 1.6 broadcast_in_dim.15.clone
  4.0 659.0 %while.17 = (s32[]{:T(128)}, f32[512,256]{0,1:T(8,128)}, f32[512,1024]{1,0:T(8,128)}, pred[]{:T(512)}, s32[]{:T(128)}, /*index=5*/f32[512,1024]{1,0:T(8,128)}, f...) while((s32[]{:T(128)}, f32[512,256]{0,1:T(8,128)}, ...), condition=%wide.region_2.3_spmd, body=%wide.region_0.2_spmd.sunk | while | flops 25771507712 | bytes 81318760 | solution.py:82
  5.4 2.1 collective-permute-start
  7.5 13.6 %collective-permute-done = f32[512,256]{0,1:T(8,128)S(1)} collective-permute-done((f32[512,256]{0,1:T(8,128)S(1)}, f32[512,256]{0,1:T(8,128)S(1)}, u32[]{:S(2)}, u32[]{:S(2)}) %collective-permute-start) | collective-permute-done | bytes 524320 | tf_op jit(solution)/shard_map/while/body/eval_jaxpr/ppermute | solution.py:53
  21.0 4.2 collective-permute-start.4
  25.2 17.5 %collective-permute-done.1 = f32[512,256]{0,1:T(8,128)S(1)} collective-permute-done((f32[512,256]{0,1:T(8,128)S(1)}, f32[512,256]{0,1:T(8,128)S(1)}, u32[]{:S(2)}, u32[]{:S(2)}) %collective-permute-start.1) | collective-permute-done | bytes 524320 | tf_op jit(solution)/shard_map/while/body/eval_jaxpr/ppermute | solution.py:53
  42.7 2.2 collective-permute-start.2
  44.9 13.5 %collective-permute-start.5 = (f32[512,256]{0,1:T(8,128)S(1)}, f32[512,256]{0,1:T(8,128)S(1)}, u32[]{:S(2)}, u32[]{:S(2)}) collective-permute-start(f32[512,256]{0,1:T(8,128)S(1)} %collective-permute-done.4), channel_id=1, source_target_pairs={{0,14},{2,0},{4,2},{6,4},{8,6},{10,8},{12,10},{14,12},{1,15},{3,1}... | collective-permute-start | bytes 1572872 | tf_op jit(solution)/shard_map/while/body/eval_jaxpr/ppermute | solution.py:56
  58.4 8.4 %collective-permute-done.2 = f32[512,256]{0,1:T(8,128)S(1)} collective-permute-done((f32[512,256]{0,1:T(8,128)S(1)}, f32[512,256]{0,1:T(8,128)S(1)}, u32[]{:S(2)}, u32[]{:S(2)}) %collective-permute-start.2) | collective-permute-done | bytes 524320 | tf_op jit(solution)/shard_map/while/body/eval_jaxpr/ppermute | solution.py:53
  66.7 2.2 collective-permute-start.3
  69.4 13.2 %collective-permute-start.6 = (f32[512,256]{0,1:T(8,128)S(1)}, f32[512,256]{0,1:T(8,128)S(1)}, u32[]{:S(2)}, u32[]{:S(2)}) collective-permute-start(f32[512,256]{0,1:T(8,128)S(1)} %collective-permute-done.5), channel_id=1, source_target_pairs={{0,14},{2,0},{4,2},{6,4},{8,6},{10,8},{12,10},{14,12},{1,15},{3,1}... | collective-permute-start | bytes 1572872 | tf_op jit(solution)/shard_map/while/body/eval_jaxpr/ppermute | solution.py:56
  82.6 8.2 %collective-permute-done.3 = f32[512,256]{0,1:T(8,128)} collective-permute-done((f32[512,256]{0,1:T(8,128)S(1)}, f32[512,256]{0,1:T(8,128)}, u32[]{:S(2)}, u32[]{:S(2)}) %collective-permute-start.3) | collective-permute-done | bytes 524320 | tf_op jit(solution)/shard_map/while/body/eval_jaxpr/ppermute | solution.py:53
  92.1 2.3 collective-permute-done.6
  95.9 32.8 %fusion.15 = f32[512,256]{0,1:T(8,128)S(1)} fusion(f32[4,512,4096]{2,1,0:T(8,128)} %get-tuple-element.372, f32[8192,256]{0,1:T(8,128)S(1)} %constant_dynamic-update-slice_fusion.49, s32[]{:T(128)S(6)} %select_n.105, f32[4,256]{1,0:T(4,128)S(1)} %constant_dynamic-slice_fusion.7, f32[4,512]{1,0:T(4,128)S(1)} %bitcast.27), kind=kOutput, calls=%fused_computation.4.clone.1 | convolution fusion | flops 25771245568 | bytes 38285316 | tf_op jit(solution)/shard_map/while/body/eval_jaxpr/arn,nc->arc/dot_general | solution.py:29
  128.7 3.2 collective-permute-start.7
  136.8 16.1 %collective-permute-done = f32[512,256]{0,1:T(8,128)S(1)} collective-permute-done((f32[512,256]{0,1:T(8,128)S(1)}, f32[512,256]{0,1:T(8,128)S(1)}, u32[]{:S(2)}, u32[]{:S(2)}) %collective-permute-start) | collective-permute-done | bytes 524320 | tf_op jit(solution)/shard_map/while/body/eval_jaxpr/ppermute | solution.py:53
  153.0 4.2 collective-permute-start.4
  157.1 18.4 %collective-permute-done.1 = f32[512,256]{0,1:T(8,128)S(1)} collective-permute-done((f32[512,256]{0,1:T(8,128)S(1)}, f32[512,256]{0,1:T(8,128)S(1)}, u32[]{:S(2)}, u32[]{:S(2)}) %collective-permute-start.1) | collective-permute-done | bytes 524320 | tf_op jit(solution)/shard_map/while/body/eval_jaxpr/ppermute | solution.py:53
  175.5 2.2 collective-permute-start.2
  177.7 2.0 collective-permute-start.5
  179.7 20.1 %collective-permute-done.2 = f32[512,256]{0,1:T(8,128)S(1)} collective-permute-done((f32[512,256]{0,1:T(8,128)S(1)}, f32[512,256]{0,1:T(8,128)S(1)}, u32[]{:S(2)}, u32[]{:S(2)}) %collective-permute-start.2) | collective-permute-done | bytes 524320 | tf_op jit(solution)/shard_map/while/body/eval_jaxpr/ppermute | solution.py:53
  199.8 2.2 collective-permute-start.3
  202.2 1.7 collective-permute-start.6
  203.9 19.9 %collective-permute-done.3 = f32[512,256]{0,1:T(8,128)} collective-permute-done((f32[512,256]{0,1:T(8,128)S(1)}, f32[512,256]{0,1:T(8,128)}, u32[]{:S(2)}, u32[]{:S(2)}) %collective-permute-start.3) | collective-permute-done | bytes 524320 | tf_op jit(solution)/shard_map/while/body/eval_jaxpr/ppermute | solution.py:53
  225.2 1.9 collective-permute-done.6
  228.5 32.8 %fusion.15 = f32[512,256]{0,1:T(8,128)S(1)} fusion(f32[4,512,4096]{2,1,0:T(8,128)} %get-tuple-element.372, f32[8192,256]{0,1:T(8,128)S(1)} %constant_dynamic-update-slice_fusion.49, s32[]{:T(128)S(6)} %select_n.105, f32[4,256]{1,0:T(4,128)S(1)} %constant_dynamic-slice_fusion.7, f32[4,512]{1,0:T(4,128)S(1)} %bitcast.27), kind=kOutput, calls=%fused_computation.4.clone.1 | convolution fusion | flops 25771245568 | bytes 38285316 | tf_op jit(solution)/shard_map/while/body/eval_jaxpr/arn,nc->arc/dot_general | solution.py:29
  261.3 3.4 collective-permute-start.7
  268.6 1.3 collective-permute-start
  269.9 15.1 %collective-permute-done = f32[512,256]{0,1:T(8,128)S(1)} collective-permute-done((f32[512,256]{0,1:T(8,128)S(1)}, f32[512,256]{0,1:T(8,128)S(1)}, u32[]{:S(2)}, u32[]{:S(2)}) %collective-permute-start) | collective-permute-done | bytes 524320 | tf_op jit(solution)/shard_map/while/body/eval_jaxpr/ppermute | solution.py:53
  285.0 4.2 collective-permute-start.4
  289.2 18.1 %collective-permute-done.1 = f32[512,256]{0,1:T(8,128)S(1)} collective-permute-done((f32[512,256]{0,1:T(8,128)S(1)}, f32[512,256]{0,1:T(8,128)S(1)}, u32[]{:S(2)}, u32[]{:S(2)}) %collective-permute-start.1) | collective-permute-done | bytes 524320 | tf_op jit(solution)/shard_map/while/body/eval_jaxpr/ppermute | solution.py:53
  307.3 2.2 collective-permute-start.2
  309.5 2.0 collective-permute-start.5
  311.5 19.9 %collective-permute-done.2 = f32[512,256]{0,1:T(8,128)S(1)} collective-permute-done((f32[512,256]{0,1:T(8,128)S(1)}, f32[512,256]{0,1:T(8,128)S(1)}, u32[]{:S(2)}, u32[]{:S(2)}) %collective-permute-start.2) | collective-permute-done | bytes 524320 | tf_op jit(solution)/shard_map/while/body/eval_jaxpr/ppermute | solution.py:53
  331.4 2.2 collective-permute-start.3
  334.1 1.6 collective-permute-start.6
  335.6 19.9 %collective-permute-done.3 = f32[512,256]{0,1:T(8,128)} collective-permute-done((f32[512,256]{0,1:T(8,128)S(1)}, f32[512,256]{0,1:T(8,128)}, u32[]{:S(2)}, u32[]{:S(2)}) %collective-permute-start.3) | collective-permute-done | bytes 524320 | tf_op jit(solution)/shard_map/while/body/eval_jaxpr/ppermute | solution.py:53
  356.8 2.2 collective-permute-done.6
  360.5 32.8 %fusion.15 = f32[512,256]{0,1:T(8,128)S(1)} fusion(f32[4,512,4096]{2,1,0:T(8,128)} %get-tuple-element.372, f32[8192,256]{0,1:T(8,128)S(1)} %constant_dynamic-update-slice_fusion.49, s32[]{:T(128)S(6)} %select_n.105, f32[4,256]{1,0:T(4,128)S(1)} %constant_dynamic-slice_fusion.7, f32[4,512]{1,0:T(4,128)S(1)} %bitcast.27), kind=kOutput, calls=%fused_computation.4.clone.1 | convolution fusion | flops 25771245568 | bytes 38285316 | tf_op jit(solution)/shard_map/while/body/eval_jaxpr/arn,nc->arc/dot_general | solution.py:29
  393.3 3.3 collective-permute-start.7
  401.5 15.3 %collective-permute-done = f32[512,256]{0,1:T(8,128)S(1)} collective-permute-done((f32[512,256]{0,1:T(8,128)S(1)}, f32[512,256]{0,1:T(8,128)S(1)}, u32[]{:S(2)}, u32[]{:S(2)}) %collective-permute-start) | collective-permute-done | bytes 524320 | tf_op jit(solution)/shard_map/while/body/eval_jaxpr/ppermute | solution.py:53
  416.8 4.2 collective-permute-start.4
  421.0 18.3 %collective-permute-done.1 = f32[512,256]{0,1:T(8,128)S(1)} collective-permute-done((f32[512,256]{0,1:T(8,128)S(1)}, f32[512,256]{0,1:T(8,128)S(1)}, u32[]{:S(2)}, u32[]{:S(2)}) %collective-permute-start.1) | collective-permute-done | bytes 524320 | tf_op jit(solution)/shard_map/while/body/eval_jaxpr/ppermute | solution.py:53
  439.3 2.2 collective-permute-start.2
  441.5 2.0 collective-permute-start.5
  443.5 20.0 %collective-permute-done.2 = f32[512,256]{0,1:T(8,128)S(1)} collective-permute-done((f32[512,256]{0,1:T(8,128)S(1)}, f32[512,256]{0,1:T(8,128)S(1)}, u32[]{:S(2)}, u32[]{:S(2)}) %collective-permute-start.2) | collective-permute-done | bytes 524320 | tf_op jit(solution)/shard_map/while/body/eval_jaxpr/ppermute | solution.py:53
  463.4 2.2 collective-permute-start.3
  466.0 1.6 collective-permute-start.6
  467.6 19.9 %collective-permute-done.3 = f32[512,256]{0,1:T(8,128)} collective-permute-done((f32[512,256]{0,1:T(8,128)S(1)}, f32[512,256]{0,1:T(8,128)}, u32[]{:S(2)}, u32[]{:S(2)}) %collective-permute-start.3) | collective-permute-done | bytes 524320 | tf_op jit(solution)/shard_map/while/body/eval_jaxpr/ppermute | solution.py:53
  488.8 2.2 collective-permute-done.6
  492.5 32.8 %fusion.15 = f32[512,256]{0,1:T(8,128)S(1)} fusion(f32[4,512,4096]{2,1,0:T(8,128)} %get-tuple-element.372, f32[8192,256]{0,1:T(8,128)S(1)} %constant_dynamic-update-slice_fusion.49, s32[]{:T(128)S(6)} %select_n.105, f32[4,256]{1,0:T(4,128)S(1)} %constant_dynamic-slice_fusion.7, f32[4,512]{1,0:T(4,128)S(1)} %bitcast.27), kind=kOutput, calls=%fused_computation.4.clone.1 | convolution fusion | flops 25771245568 | bytes 38285316 | tf_op jit(solution)/shard_map/while/body/eval_jaxpr/arn,nc->arc/dot_general | solution.py:29
  525.3 3.3 collective-permute-start.7
  533.5 15.3 %collective-permute-done = f32[512,256]{0,1:T(8,128)S(1)} collective-permute-done((f32[512,256]{0,1:T(8,128)S(1)}, f32[512,256]{0,1:T(8,128)S(1)}, u32[]{:S(2)}, u32[]{:S(2)}) %collective-permute-start) | collective-permute-done | bytes 524320 | tf_op jit(solution)/shard_map/while/body/eval_jaxpr/ppermute | solution.py:53
  548.8 4.2 collective-permute-start.4
  553.0 18.3 %collective-permute-done.1 = f32[512,256]{0,1:T(8,128)S(1)} collective-permute-done((f32[512,256]{0,1:T(8,128)S(1)}, f32[512,256]{0,1:T(8,128)S(1)}, u32[]{:S(2)}, u32[]{:S(2)}) %collective-permute-start.1) | collective-permute-done | bytes 524320 | tf_op jit(solution)/shard_map/while/body/eval_jaxpr/ppermute | solution.py:53
  571.3 2.2 collective-permute-start.2
  573.5 2.0 collective-permute-start.5
  575.4 20.0 %collective-permute-done.2 = f32[512,256]{0,1:T(8,128)S(1)} collective-permute-done((f32[512,256]{0,1:T(8,128)S(1)}, f32[512,256]{0,1:T(8,128)S(1)}, u32[]{:S(2)}, u32[]{:S(2)}) %collective-permute-start.2) | collective-permute-done | bytes 524320 | tf_op jit(solution)/shard_map/while/body/eval_jaxpr/ppermute | solution.py:53
  595.4 2.2 collective-permute-start.3
  598.0 1.6 collective-permute-start.6
  599.6 19.9 %collective-permute-done.3 = f32[512,256]{0,1:T(8,128)} collective-permute-done((f32[512,256]{0,1:T(8,128)S(1)}, f32[512,256]{0,1:T(8,128)}, u32[]{:S(2)}, u32[]{:S(2)}) %collective-permute-start.3) | collective-permute-done | bytes 524320 | tf_op jit(solution)/shard_map/while/body/eval_jaxpr/ppermute | solution.py:53
  620.8 2.2 collective-permute-done.6
  624.4 32.8 %fusion.15 = f32[512,256]{0,1:T(8,128)S(1)} fusion(f32[4,512,4096]{2,1,0:T(8,128)} %get-tuple-element.372, f32[8192,256]{0,1:T(8,128)S(1)} %constant_dynamic-update-slice_fusion.49, s32[]{:T(128)S(6)} %select_n.105, f32[4,256]{1,0:T(4,128)S(1)} %constant_dynamic-slice_fusion.7, f32[4,512]{1,0:T(4,128)S(1)} %bitcast.27), kind=kOutput, calls=%fused_computation.4.clone.1 | convolution fusion | flops 25771245568 | bytes 38285316 | tf_op jit(solution)/shard_map/while/body/eval_jaxpr/arn,nc->arc/dot_general | solution.py:29
  657.3 3.3 collective-permute-start.7
  (162 shorter events, 39.8 us)
Async XLA Ops:
  0.0 0.7 copy-start
  5.4 15.7 %collective-permute-start = (f32[512,256]{0,1:T(8,128)S(1)}, f32[512,256]{0,1:T(8,128)S(1)}, u32[]{:S(2)}, u32[]{:S(2)}) collective-permute-start(f32[512,256]{0,1:T(8,128)S(1)} %broadcast_select_fusion.4), channel_id=1, source_target_pairs={{0,2},{2,4},{4,6},{6,8},{8,10},{10,12},{12,14},{14,0},{1,3},{3,5},... | collective-permute-start | bytes 1572872 | tf_op jit(solution)/shard_map/while/body/eval_jaxpr/ppermute | solution.py:53
  21.0 21.6 %collective-permute-start.1 = (f32[512,256]{0,1:T(8,128)S(1)}, f32[512,256]{0,1:T(8,128)S(1)}, u32[]{:S(2)}, u32[]{:S(2)}) collective-permute-start(f32[512,256]{0,1:T(8,128)S(1)} %collective-permute-done), channel_id=1, source_target_pairs={{0,2},{2,4},{4,6},{6,8},{8,10},{10,12},{12,14},{14,0},{1,3},{3,5},... | collective-permute-start | bytes 1572872 | tf_op jit(solution)/shard_map/while/body/eval_jaxpr/ppermute | solution.py:53
  21.0 23.8 %collective-permute-start.4 = (f32[512,256]{0,1:T(8,128)S(1)}, f32[512,256]{0,1:T(8,128)S(1)}, u32[]{:S(2)}, u32[]{:S(2)}) collective-permute-start(f32[512,256]{0,1:T(8,128)S(1)} %broadcast_select_fusion.4), channel_id=1, source_target_pairs={{0,14},{2,0},{4,2},{6,4},{8,6},{10,8},{12,10},{14,12},{1,15},{3,1}... | collective-permute-start | bytes 1572872 | tf_op jit(solution)/shard_map/while/body/eval_jaxpr/ppermute | solution.py:56
  42.7 24.1 %collective-permute-start.2 = (f32[512,256]{0,1:T(8,128)S(1)}, f32[512,256]{0,1:T(8,128)S(1)}, u32[]{:S(2)}, u32[]{:S(2)}) collective-permute-start(f32[512,256]{0,1:T(8,128)S(1)} %collective-permute-done.1), channel_id=1, source_target_pairs={{0,2},{2,4},{4,6},{6,8},{8,10},{10,12},{12,14},{14,0},{1,3},{3,5},... | collective-permute-start | bytes 1572872 | tf_op jit(solution)/shard_map/while/body/eval_jaxpr/ppermute | solution.py:53
  44.9 24.5 %collective-permute-start.5 = (f32[512,256]{0,1:T(8,128)S(1)}, f32[512,256]{0,1:T(8,128)S(1)}, u32[]{:S(2)}, u32[]{:S(2)}) collective-permute-start(f32[512,256]{0,1:T(8,128)S(1)} %collective-permute-done.4), channel_id=1, source_target_pairs={{0,14},{2,0},{4,2},{6,4},{8,6},{10,8},{12,10},{14,12},{1,15},{3,1}... | collective-permute-start | bytes 1572872 | tf_op jit(solution)/shard_map/while/body/eval_jaxpr/ppermute | solution.py:56
  66.7 24.0 %collective-permute-start.3 = (f32[512,256]{0,1:T(8,128)S(1)}, f32[512,256]{0,1:T(8,128)}, u32[]{:S(2)}, u32[]{:S(2)}) collective-permute-start(f32[512,256]{0,1:T(8,128)S(1)} %collective-permute-done.2), channel_id=1, source_target_pairs={{0,2},{2,4},{4,6},{6,8},{8,10},{10,12},{12,14},{14,0},{1,3},{3,5},... | collective-permute-start | bytes 1572872 | tf_op jit(solution)/shard_map/while/body/eval_jaxpr/ppermute | solution.py:53
  68.9 27.0 %copy-start.1 = (f32[1,4,512]{2,1,0:T(4,128)S(1)}, f32[1,4,512]{2,1,0:T(4,128)}, u32[]{:S(2)}) copy-start(f32[1,4,512]{2,1,0:T(4,128)} %get-tuple-element.373) | copy-start | bytes 24580 | tf_op jit(solution)/shard_map/while
  69.4 25.1 %collective-permute-start.6 = (f32[512,256]{0,1:T(8,128)S(1)}, f32[512,256]{0,1:T(8,128)S(1)}, u32[]{:S(2)}, u32[]{:S(2)}) collective-permute-start(f32[512,256]{0,1:T(8,128)S(1)} %collective-permute-done.5), channel_id=1, source_target_pairs={{0,14},{2,0},{4,2},{6,4},{8,6},{10,8},{12,10},{14,12},{1,15},{3,1}... | collective-permute-start | bytes 1572872 | tf_op jit(solution)/shard_map/while/body/eval_jaxpr/ppermute | solution.py:56
  128.7 5.7 collective-permute-start.7
  135.8 17.2 %collective-permute-start = (f32[512,256]{0,1:T(8,128)S(1)}, f32[512,256]{0,1:T(8,128)S(1)}, u32[]{:S(2)}, u32[]{:S(2)}) collective-permute-start(f32[512,256]{0,1:T(8,128)S(1)} %broadcast_select_fusion.4), channel_id=1, source_target_pairs={{0,2},{2,4},{4,6},{6,8},{8,10},{10,12},{12,14},{14,0},{1,3},{3,5},... | collective-permute-start | bytes 1572872 | tf_op jit(solution)/shard_map/while/body/eval_jaxpr/ppermute | solution.py:53
  153.0 22.5 %collective-permute-start.1 = (f32[512,256]{0,1:T(8,128)S(1)}, f32[512,256]{0,1:T(8,128)S(1)}, u32[]{:S(2)}, u32[]{:S(2)}) collective-permute-start(f32[512,256]{0,1:T(8,128)S(1)} %collective-permute-done), channel_id=1, source_target_pairs={{0,2},{2,4},{4,6},{6,8},{8,10},{10,12},{12,14},{14,0},{1,3},{3,5},... | collective-permute-start | bytes 1572872 | tf_op jit(solution)/shard_map/while/body/eval_jaxpr/ppermute | solution.py:53
  153.0 24.7 %collective-permute-start.4 = (f32[512,256]{0,1:T(8,128)S(1)}, f32[512,256]{0,1:T(8,128)S(1)}, u32[]{:S(2)}, u32[]{:S(2)}) collective-permute-start(f32[512,256]{0,1:T(8,128)S(1)} %broadcast_select_fusion.4), channel_id=1, source_target_pairs={{0,14},{2,0},{4,2},{6,4},{8,6},{10,8},{12,10},{14,12},{1,15},{3,1}... | collective-permute-start | bytes 1572872 | tf_op jit(solution)/shard_map/while/body/eval_jaxpr/ppermute | solution.py:56
  175.5 24.3 %collective-permute-start.2 = (f32[512,256]{0,1:T(8,128)S(1)}, f32[512,256]{0,1:T(8,128)S(1)}, u32[]{:S(2)}, u32[]{:S(2)}) collective-permute-start(f32[512,256]{0,1:T(8,128)S(1)} %collective-permute-done.1), channel_id=1, source_target_pairs={{0,2},{2,4},{4,6},{6,8},{8,10},{10,12},{12,14},{14,0},{1,3},{3,5},... | collective-permute-start | bytes 1572872 | tf_op jit(solution)/shard_map/while/body/eval_jaxpr/ppermute | solution.py:53
  177.7 24.5 %collective-permute-start.5 = (f32[512,256]{0,1:T(8,128)S(1)}, f32[512,256]{0,1:T(8,128)S(1)}, u32[]{:S(2)}, u32[]{:S(2)}) collective-permute-start(f32[512,256]{0,1:T(8,128)S(1)} %collective-permute-done.4), channel_id=1, source_target_pairs={{0,14},{2,0},{4,2},{6,4},{8,6},{10,8},{12,10},{14,12},{1,15},{3,1}... | collective-permute-start | bytes 1572872 | tf_op jit(solution)/shard_map/while/body/eval_jaxpr/ppermute | solution.py:56
  199.8 24.0 %collective-permute-start.3 = (f32[512,256]{0,1:T(8,128)S(1)}, f32[512,256]{0,1:T(8,128)}, u32[]{:S(2)}, u32[]{:S(2)}) collective-permute-start(f32[512,256]{0,1:T(8,128)S(1)} %collective-permute-done.2), channel_id=1, source_target_pairs={{0,2},{2,4},{4,6},{6,8},{8,10},{10,12},{12,14},{14,0},{1,3},{3,5},... | collective-permute-start | bytes 1572872 | tf_op jit(solution)/shard_map/while/body/eval_jaxpr/ppermute | solution.py:53
  202.0 26.5 %copy-start.1 = (f32[1,4,512]{2,1,0:T(4,128)S(1)}, f32[1,4,512]{2,1,0:T(4,128)}, u32[]{:S(2)}) copy-start(f32[1,4,512]{2,1,0:T(4,128)} %get-tuple-element.373) | copy-start | bytes 24580 | tf_op jit(solution)/shard_map/while
  202.2 24.8 %collective-permute-start.6 = (f32[512,256]{0,1:T(8,128)S(1)}, f32[512,256]{0,1:T(8,128)S(1)}, u32[]{:S(2)}, u32[]{:S(2)}) collective-permute-start(f32[512,256]{0,1:T(8,128)S(1)} %collective-permute-done.5), channel_id=1, source_target_pairs={{0,14},{2,0},{4,2},{6,4},{8,6},{10,8},{12,10},{14,12},{1,15},{3,1}... | collective-permute-start | bytes 1572872 | tf_op jit(solution)/shard_map/while/body/eval_jaxpr/ppermute | solution.py:56
  261.3 5.9 collective-permute-start.7
  268.6 16.4 %collective-permute-start = (f32[512,256]{0,1:T(8,128)S(1)}, f32[512,256]{0,1:T(8,128)S(1)}, u32[]{:S(2)}, u32[]{:S(2)}) collective-permute-start(f32[512,256]{0,1:T(8,128)S(1)} %broadcast_select_fusion.4), channel_id=1, source_target_pairs={{0,2},{2,4},{4,6},{6,8},{8,10},{10,12},{12,14},{14,0},{1,3},{3,5},... | collective-permute-start | bytes 1572872 | tf_op jit(solution)/shard_map/while/body/eval_jaxpr/ppermute | solution.py:53
  285.0 22.3 %collective-permute-start.1 = (f32[512,256]{0,1:T(8,128)S(1)}, f32[512,256]{0,1:T(8,128)S(1)}, u32[]{:S(2)}, u32[]{:S(2)}) collective-permute-start(f32[512,256]{0,1:T(8,128)S(1)} %collective-permute-done), channel_id=1, source_target_pairs={{0,2},{2,4},{4,6},{6,8},{8,10},{10,12},{12,14},{14,0},{1,3},{3,5},... | collective-permute-start | bytes 1572872 | tf_op jit(solution)/shard_map/while/body/eval_jaxpr/ppermute | solution.py:53
  285.0 24.5 %collective-permute-start.4 = (f32[512,256]{0,1:T(8,128)S(1)}, f32[512,256]{0,1:T(8,128)S(1)}, u32[]{:S(2)}, u32[]{:S(2)}) collective-permute-start(f32[512,256]{0,1:T(8,128)S(1)} %broadcast_select_fusion.4), channel_id=1, source_target_pairs={{0,14},{2,0},{4,2},{6,4},{8,6},{10,8},{12,10},{14,12},{1,15},{3,1}... | collective-permute-start | bytes 1572872 | tf_op jit(solution)/shard_map/while/body/eval_jaxpr/ppermute | solution.py:56
  307.3 24.1 %collective-permute-start.2 = (f32[512,256]{0,1:T(8,128)S(1)}, f32[512,256]{0,1:T(8,128)S(1)}, u32[]{:S(2)}, u32[]{:S(2)}) collective-permute-start(f32[512,256]{0,1:T(8,128)S(1)} %collective-permute-done.1), channel_id=1, source_target_pairs={{0,2},{2,4},{4,6},{6,8},{8,10},{10,12},{12,14},{14,0},{1,3},{3,5},... | collective-permute-start | bytes 1572872 | tf_op jit(solution)/shard_map/while/body/eval_jaxpr/ppermute | solution.py:53
  309.5 24.5 %collective-permute-start.5 = (f32[512,256]{0,1:T(8,128)S(1)}, f32[512,256]{0,1:T(8,128)S(1)}, u32[]{:S(2)}, u32[]{:S(2)}) collective-permute-start(f32[512,256]{0,1:T(8,128)S(1)} %collective-permute-done.4), channel_id=1, source_target_pairs={{0,14},{2,0},{4,2},{6,4},{8,6},{10,8},{12,10},{14,12},{1,15},{3,1}... | collective-permute-start | bytes 1572872 | tf_op jit(solution)/shard_map/while/body/eval_jaxpr/ppermute | solution.py:56
  331.4 24.0 %collective-permute-start.3 = (f32[512,256]{0,1:T(8,128)S(1)}, f32[512,256]{0,1:T(8,128)}, u32[]{:S(2)}, u32[]{:S(2)}) collective-permute-start(f32[512,256]{0,1:T(8,128)S(1)} %collective-permute-done.2), channel_id=1, source_target_pairs={{0,2},{2,4},{4,6},{6,8},{8,10},{10,12},{12,14},{14,0},{1,3},{3,5},... | collective-permute-start | bytes 1572872 | tf_op jit(solution)/shard_map/while/body/eval_jaxpr/ppermute | solution.py:53
  333.6 26.9 %copy-start.1 = (f32[1,4,512]{2,1,0:T(4,128)S(1)}, f32[1,4,512]{2,1,0:T(4,128)}, u32[]{:S(2)}) copy-start(f32[1,4,512]{2,1,0:T(4,128)} %get-tuple-element.373) | copy-start | bytes 24580 | tf_op jit(solution)/shard_map/while
  334.1 25.0 %collective-permute-start.6 = (f32[512,256]{0,1:T(8,128)S(1)}, f32[512,256]{0,1:T(8,128)S(1)}, u32[]{:S(2)}, u32[]{:S(2)}) collective-permute-start(f32[512,256]{0,1:T(8,128)S(1)} %collective-permute-done.5), channel_id=1, source_target_pairs={{0,14},{2,0},{4,2},{6,4},{8,6},{10,8},{12,10},{14,12},{1,15},{3,1}... | collective-permute-start | bytes 1572872 | tf_op jit(solution)/shard_map/while/body/eval_jaxpr/ppermute | solution.py:56
  393.3 5.7 collective-permute-start.7
  400.4 16.4 %collective-permute-start = (f32[512,256]{0,1:T(8,128)S(1)}, f32[512,256]{0,1:T(8,128)S(1)}, u32[]{:S(2)}, u32[]{:S(2)}) collective-permute-start(f32[512,256]{0,1:T(8,128)S(1)} %broadcast_select_fusion.4), channel_id=1, source_target_pairs={{0,2},{2,4},{4,6},{6,8},{8,10},{10,12},{12,14},{14,0},{1,3},{3,5},... | collective-permute-start | bytes 1572872 | tf_op jit(solution)/shard_map/while/body/eval_jaxpr/ppermute | solution.py:53
  416.8 22.5 %collective-permute-start.1 = (f32[512,256]{0,1:T(8,128)S(1)}, f32[512,256]{0,1:T(8,128)S(1)}, u32[]{:S(2)}, u32[]{:S(2)}) collective-permute-start(f32[512,256]{0,1:T(8,128)S(1)} %collective-permute-done), channel_id=1, source_target_pairs={{0,2},{2,4},{4,6},{6,8},{8,10},{10,12},{12,14},{14,0},{1,3},{3,5},... | collective-permute-start | bytes 1572872 | tf_op jit(solution)/shard_map/while/body/eval_jaxpr/ppermute | solution.py:53
  416.8 24.7 %collective-permute-start.4 = (f32[512,256]{0,1:T(8,128)S(1)}, f32[512,256]{0,1:T(8,128)S(1)}, u32[]{:S(2)}, u32[]{:S(2)}) collective-permute-start(f32[512,256]{0,1:T(8,128)S(1)} %broadcast_select_fusion.4), channel_id=1, source_target_pairs={{0,14},{2,0},{4,2},{6,4},{8,6},{10,8},{12,10},{14,12},{1,15},{3,1}... | collective-permute-start | bytes 1572872 | tf_op jit(solution)/shard_map/while/body/eval_jaxpr/ppermute | solution.py:56
  439.3 24.1 %collective-permute-start.2 = (f32[512,256]{0,1:T(8,128)S(1)}, f32[512,256]{0,1:T(8,128)S(1)}, u32[]{:S(2)}, u32[]{:S(2)}) collective-permute-start(f32[512,256]{0,1:T(8,128)S(1)} %collective-permute-done.1), channel_id=1, source_target_pairs={{0,2},{2,4},{4,6},{6,8},{8,10},{10,12},{12,14},{14,0},{1,3},{3,5},... | collective-permute-start | bytes 1572872 | tf_op jit(solution)/shard_map/while/body/eval_jaxpr/ppermute | solution.py:53
  441.5 24.5 %collective-permute-start.5 = (f32[512,256]{0,1:T(8,128)S(1)}, f32[512,256]{0,1:T(8,128)S(1)}, u32[]{:S(2)}, u32[]{:S(2)}) collective-permute-start(f32[512,256]{0,1:T(8,128)S(1)} %collective-permute-done.4), channel_id=1, source_target_pairs={{0,14},{2,0},{4,2},{6,4},{8,6},{10,8},{12,10},{14,12},{1,15},{3,1}... | collective-permute-start | bytes 1572872 | tf_op jit(solution)/shard_map/while/body/eval_jaxpr/ppermute | solution.py:56
  463.4 24.0 %collective-permute-start.3 = (f32[512,256]{0,1:T(8,128)S(1)}, f32[512,256]{0,1:T(8,128)}, u32[]{:S(2)}, u32[]{:S(2)}) collective-permute-start(f32[512,256]{0,1:T(8,128)S(1)} %collective-permute-done.2), channel_id=1, source_target_pairs={{0,2},{2,4},{4,6},{6,8},{8,10},{10,12},{12,14},{14,0},{1,3},{3,5},... | collective-permute-start | bytes 1572872 | tf_op jit(solution)/shard_map/while/body/eval_jaxpr/ppermute | solution.py:53
  465.6 26.8 %copy-start.1 = (f32[1,4,512]{2,1,0:T(4,128)S(1)}, f32[1,4,512]{2,1,0:T(4,128)}, u32[]{:S(2)}) copy-start(f32[1,4,512]{2,1,0:T(4,128)} %get-tuple-element.373) | copy-start | bytes 24580 | tf_op jit(solution)/shard_map/while
  466.0 25.0 %collective-permute-start.6 = (f32[512,256]{0,1:T(8,128)S(1)}, f32[512,256]{0,1:T(8,128)S(1)}, u32[]{:S(2)}, u32[]{:S(2)}) collective-permute-start(f32[512,256]{0,1:T(8,128)S(1)} %collective-permute-done.5), channel_id=1, source_target_pairs={{0,14},{2,0},{4,2},{6,4},{8,6},{10,8},{12,10},{14,12},{1,15},{3,1}... | collective-permute-start | bytes 1572872 | tf_op jit(solution)/shard_map/while/body/eval_jaxpr/ppermute | solution.py:56
  525.3 5.7 collective-permute-start.7
  532.4 16.4 %collective-permute-start = (f32[512,256]{0,1:T(8,128)S(1)}, f32[512,256]{0,1:T(8,128)S(1)}, u32[]{:S(2)}, u32[]{:S(2)}) collective-permute-start(f32[512,256]{0,1:T(8,128)S(1)} %broadcast_select_fusion.4), channel_id=1, source_target_pairs={{0,2},{2,4},{4,6},{6,8},{8,10},{10,12},{12,14},{14,0},{1,3},{3,5},... | collective-permute-start | bytes 1572872 | tf_op jit(solution)/shard_map/while/body/eval_jaxpr/ppermute | solution.py:53
  548.8 22.5 %collective-permute-start.1 = (f32[512,256]{0,1:T(8,128)S(1)}, f32[512,256]{0,1:T(8,128)S(1)}, u32[]{:S(2)}, u32[]{:S(2)}) collective-permute-start(f32[512,256]{0,1:T(8,128)S(1)} %collective-permute-done), channel_id=1, source_target_pairs={{0,2},{2,4},{4,6},{6,8},{8,10},{10,12},{12,14},{14,0},{1,3},{3,5},... | collective-permute-start | bytes 1572872 | tf_op jit(solution)/shard_map/while/body/eval_jaxpr/ppermute | solution.py:53
  548.8 24.7 %collective-permute-start.4 = (f32[512,256]{0,1:T(8,128)S(1)}, f32[512,256]{0,1:T(8,128)S(1)}, u32[]{:S(2)}, u32[]{:S(2)}) collective-permute-start(f32[512,256]{0,1:T(8,128)S(1)} %broadcast_select_fusion.4), channel_id=1, source_target_pairs={{0,14},{2,0},{4,2},{6,4},{8,6},{10,8},{12,10},{14,12},{1,15},{3,1}... | collective-permute-start | bytes 1572872 | tf_op jit(solution)/shard_map/while/body/eval_jaxpr/ppermute | solution.py:56
  571.3 24.1 %collective-permute-start.2 = (f32[512,256]{0,1:T(8,128)S(1)}, f32[512,256]{0,1:T(8,128)S(1)}, u32[]{:S(2)}, u32[]{:S(2)}) collective-permute-start(f32[512,256]{0,1:T(8,128)S(1)} %collective-permute-done.1), channel_id=1, source_target_pairs={{0,2},{2,4},{4,6},{6,8},{8,10},{10,12},{12,14},{14,0},{1,3},{3,5},... | collective-permute-start | bytes 1572872 | tf_op jit(solution)/shard_map/while/body/eval_jaxpr/ppermute | solution.py:53
  573.5 24.5 %collective-permute-start.5 = (f32[512,256]{0,1:T(8,128)S(1)}, f32[512,256]{0,1:T(8,128)S(1)}, u32[]{:S(2)}, u32[]{:S(2)}) collective-permute-start(f32[512,256]{0,1:T(8,128)S(1)} %collective-permute-done.4), channel_id=1, source_target_pairs={{0,14},{2,0},{4,2},{6,4},{8,6},{10,8},{12,10},{14,12},{1,15},{3,1}... | collective-permute-start | bytes 1572872 | tf_op jit(solution)/shard_map/while/body/eval_jaxpr/ppermute | solution.py:56
  595.4 24.0 %collective-permute-start.3 = (f32[512,256]{0,1:T(8,128)S(1)}, f32[512,256]{0,1:T(8,128)}, u32[]{:S(2)}, u32[]{:S(2)}) collective-permute-start(f32[512,256]{0,1:T(8,128)S(1)} %collective-permute-done.2), channel_id=1, source_target_pairs={{0,2},{2,4},{4,6},{6,8},{8,10},{10,12},{12,14},{14,0},{1,3},{3,5},... | collective-permute-start | bytes 1572872 | tf_op jit(solution)/shard_map/while/body/eval_jaxpr/ppermute | solution.py:53
  597.6 26.8 %copy-start.1 = (f32[1,4,512]{2,1,0:T(4,128)S(1)}, f32[1,4,512]{2,1,0:T(4,128)}, u32[]{:S(2)}) copy-start(f32[1,4,512]{2,1,0:T(4,128)} %get-tuple-element.373) | copy-start | bytes 24580 | tf_op jit(solution)/shard_map/while
  598.0 25.0 %collective-permute-start.6 = (f32[512,256]{0,1:T(8,128)S(1)}, f32[512,256]{0,1:T(8,128)S(1)}, u32[]{:S(2)}, u32[]{:S(2)}) collective-permute-start(f32[512,256]{0,1:T(8,128)S(1)} %collective-permute-done.5), channel_id=1, source_target_pairs={{0,14},{2,0},{4,2},{6,4},{8,6},{10,8},{12,10},{14,12},{1,15},{3,1}... | collective-permute-start | bytes 1572872 | tf_op jit(solution)/shard_map/while/body/eval_jaxpr/ppermute | solution.py:56
  657.3 5.7 collective-permute-start.7
